TPU v7x, 32 devices: a whole 2x2x4 slice. The times are simulated.
32 devices in a mesh: grp: 4 (over y, x), sub: 8 (over z, core).
Axes of the slice: x: 2, y: 2, z: 4, core: 2. Of those that a mesh axis runs over, the one named last changes fastest.
Arguments:
- residual: bfloat16 [4, 8, 1024, 2048], P('grp', 'sub'), may hold values from -6 to 6
- inverse_blocks: bfloat16 [4, 8, 1024, 1536], P('grp', 'sub'), may hold values from -0.15625 to 0.15625
- operator_tiles: bfloat16 [4, 8, 8, 8, 128, 128], P('grp', 'sub'), may hold values from -0.1875 to 0.1875
- column_blocks: int32 [4, 8, 8, 8], P('grp', 'sub'), may hold values from 0 to 11
- coarse_basis: bfloat16 [4, 8, 1024, 200], P('grp', 'sub'), may hold values from -6 to 6
- face_rows: int32 [4, 8, 4, 128], P('grp', 'sub'), may hold values from 0 to 1023
Outputs:
- local_fix: bfloat16 [4, 8, 1024, 2048], P('grp', 'sub')
- galerkin: float32 [200, 200], replicated
- coarse_rhs: float32 [200, 2048], P(None, 'sub')
All inputs are finite; a program needn't handle non-finite values.
Results may differ from a plain program's by a relative error of at most 0.0029.
Values may be sent and summed in bfloat16 or wider, within the bound.
A program may use at most 128 MiB of HBM per device.

v0:
```python
import math
import jax
import jax.numpy as jnp
from jax import lax
from jax.sharding import PartitionSpec as P


def passed_along(x, axis, by):
    devices = lax.axis_size(axis)
    pairs = [(i, i + by) for i in range(devices) if 0 <= i + by < devices]
    return lax.ppermute(x, axis, pairs)


def local(residual, inverse_blocks, operator_tiles, column_blocks, coarse_basis, face_rows):
    resid_own = residual[0, 0]
    basis_own = coarse_basis[0, 0]
    rows_here = face_rows[0, 0]
    resid_face = [jnp.take(resid_own, rows_here[face_index], axis=0) for face_index in range(4)]
    basis_face = [jnp.take(basis_own, rows_here[face_index], axis=0) for face_index in range(4)]
    from_grp_low = passed_along((resid_face[0], basis_face[0]), "grp", 1)
    from_grp_high = passed_along((resid_face[1], basis_face[1]), "grp", -1)
    from_sub_low = passed_along((resid_face[2], basis_face[2]), "sub", 1)
    from_sub_high = passed_along((resid_face[3], basis_face[3]), "sub", -1)
    rhs_term = jnp.einsum("rc,rk->ck", basis_own, resid_own, preferred_element_type=jnp.float32)
    resid_ext = jnp.concatenate(
        [resid_own, from_grp_low[0], from_grp_high[0], from_sub_low[0], from_sub_high[0]], axis=0
    )
    basis_ext = jnp.concatenate(
        [basis_own, from_grp_low[1], from_grp_high[1], from_sub_low[1], from_sub_high[1]], axis=0
    )
    correction = jnp.dot(
        inverse_blocks[0, 0], resid_ext, preferred_element_type=jnp.float32
    ).astype(jnp.bfloat16)
    tile_size = operator_tiles.shape[-1]
    coarse_width = basis_own.shape[1]
    blocks = basis_ext.reshape(-1, tile_size, coarse_width)
    picked = jnp.take(blocks, column_blocks[0, 0], axis=0)
    applied = jnp.einsum(
        "bjtu,bjuc->btc", operator_tiles[0, 0], picked, preferred_element_type=jnp.float32
    )
    applied = applied.reshape(-1, coarse_width).astype(jnp.bfloat16)
    galerkin_term = jnp.einsum("rc,rd->cd", basis_own, applied, preferred_element_type=jnp.float32)
    group_count = lax.axis_size("grp")
    sub_count = lax.axis_size("sub")
    scaling = 1.0 / math.sqrt(resid_own.shape[0] * group_count * sub_count)
    galerkin = lax.psum(galerkin_term, ("grp", "sub")) * scaling
    partial_rhs = lax.psum_scatter(rhs_term, "sub", scatter_dimension=1, tiled=True)
    owned = lax.psum(partial_rhs, "grp")
    coarse_rhs = owned * scaling
    return (correction[None, None], galerkin, coarse_rhs)


def solution(mesh):
    return jax.shard_map(
        local,
        mesh=mesh,
        in_specs=(
            P("grp", "sub", None, None),
            P("grp", "sub", None, None),
            P("grp", "sub", None, None, None, None),
            P("grp", "sub", None, None),
            P("grp", "sub", None, None),
            P("grp", "sub", None, None),
        ),
        out_specs=(P("grp", "sub", None, None), P(), P(None, "sub")),
        check_vma=False,
    )
```

profile of v0, /device:TPU:0, one launch (start us, length us, event | category | flops | bytes accessed | tf_op | source)
XLA Modules:
  0.0 243.4 jit_solution(386409287082498284)
XLA Ops:
  8.1 0.9 compare_and_fusion.1
  9.0 2.0 copy.13
  11.1 1.9 gather_fusion.5
  12.9 0.1 broadcast_select_fusion.7
  13.0 4.9 %collective-permute-start.4 = (bf16[128,200]{1,0:T(8,128)(2,1)S(1)}, bf16[128,200]{1,0:T(8,128)(2,1)S(1)}, u32[]{:S(2)}, u32[]{:S(2)}) collective-permute-start(bf16[128,200]{1,0:T(8,128)(2,1)S(1)} %broadcast_select_fusion.7), channel_id=1, source_target_pairs={{0,8},{8,16},{16,24},{1,9},{9,17},{17,25},{2,10},{10,18},{18,26},{... | collective-permute-start | bytes 153608 | tf_op jit(solution)/shard_map/ppermute | solution.py:11
  17.9 1.9 gather_fusion.6
  19.8 0.1 broadcast_select_fusion.6
  19.9 1.3 collective-permute-start.5
  21.3 1.9 gather_fusion.7
  23.2 2.1 collective-permute-start.6
  25.3 1.9 gather_fusion.8
  27.2 0.7 broadcast_select_fusion.4
  27.9 1.3 collective-permute-start.7
  29.2 1.9 constant_dynamic-update-slice_fusion.9
  31.1 0.6 compare_and_fusion
  31.8 0.6 constant_dynamic-update-slice_fusion.8
  32.4 0.6 constant_dynamic-update-slice_fusion.7
  33.1 1.5 constant_dynamic-update-slice_fusion.6
  34.6 0.6 constant_dynamic-update-slice_fusion.5
  35.2 4.0 %gather_fusion = bf16[64,128,200]{2,1,0:T(8,128)(2,1)} fusion(bf16[12,128,200]{2,1,0:T(8,128)(2,1)} %bitcast.70, s32[1024]{0:T(1024)S(1)} %pad_clamp_fusion), kind=kCustom, calls=%fused_computation.8 | custom fusion | bytes 6553856 | tf_op jit(solution)/shard_map/jit(_take)/gather | solution.py:37
  39.1 6.0 %copy.14 = bf16[64,128,200]{1,2,0:T(8,128)(2,1)} copy(bf16[64,128,200]{2,1,0:T(8,128)(2,1)} %gather_fusion) | data formatting | bytes 6553600 | tf_op jit(solution)/shard_map/jit(_take)/gather | solution.py:37
  45.2 3.7 %fusion.16 = bf16[8,25,8,128]{3,2,1,0:T(8,128)(2,1)S(1)} fusion(bf16[1,1,8,8,128,128]{5,4,3,2,1,0:T(8,128)(2,1)} %param.12, bf16[8,8,128,200]{2,3,1,0:T(8,128)(2,1)} %bitcast.75, pred[8,8]{1,0:T(8,128)(4,1)} %compare_and_fusion), kind=kOutput, calls=%fused_computation.18 | convolution fusion | flops 421273600 | bytes 5783616 | tf_op jit(solution)/shard_map/bjtu,bjuc->btc/dot_general | solution.py:38
  48.9 1.0 convolution_bitcast_fusion
  49.9 4.4 %fusion.23 = f32[200,2048]{1,0:T(8,128)} fusion(bf16[1,1,1024,200]{2,3,1,0:T(8,128)(2,1)S(1)} %copy-done.1, bf16[1,1,1024,2048]{3,2,1,0:T(8,128)(2,1)} %param.10), kind=kOutput, calls=%fused_computation.26 | convolution fusion | flops 838860800 | bytes 6242304 | tf_op jit(solution)/shard_map/rc,rk->ck/dot_general | solution.py:24
  54.4 5.1 %gather_fusion.1 = bf16[128,2048]{1,0:T(8,128)(2,1)} fusion(bf16[1024,2048]{1,0:T(8,128)(2,1)} %bitcast.66, s32[1024]{0:T(1024)} %copy-done.3), kind=kCustom, calls=%fused_computation.clone | custom fusion | bytes 1049088 | tf_op jit(solution)/shard_map/jit(_take)/gather | solution.py:18
  59.5 2.0 broadcast_select_fusion.3
  61.5 5.3 %collective-permute-start = (bf16[128,2048]{1,0:T(8,128)(2,1)}, bf16[128,2048]{1,0:T(8,128)(2,1)}, u32[]{:S(2)}, u32[]{:S(2)}) collective-permute-start(bf16[128,2048]{1,0:T(8,128)(2,1)} %broadcast_select_fusion.3), channel_id=1, source_target_pairs={{0,8},{8,16},{16,24},{1,9},{9,17},{17,25},{2,10},{10,18},{18,26},{... | collective-permute-start | bytes 1572872 | tf_op jit(solution)/shard_map/ppermute | solution.py:11
  66.8 5.2 %gather_fusion.2 = bf16[128,2048]{1,0:T(8,128)(2,1)} fusion(bf16[1024,2048]{1,0:T(8,128)(2,1)} %bitcast.67, s32[1024]{0:T(1024)} %copy-done.4), kind=kCustom, calls=%fused_computation.2.clone | custom fusion | bytes 1049088 | tf_op jit(solution)/shard_map/jit(_take)/gather | solution.py:18
  72.0 2.0 broadcast_select_fusion.2
  74.0 1.4 collective-permute-start.1
  75.4 5.1 %gather_fusion.3 = bf16[128,2048]{1,0:T(8,128)(2,1)} fusion(bf16[1024,2048]{1,0:T(8,128)(2,1)} %bitcast.68, s32[1024]{0:T(1024)} %copy-done.5), kind=kCustom, calls=%fused_computation.3.clone | custom fusion | bytes 1049088 | tf_op jit(solution)/shard_map/jit(_take)/gather | solution.py:18
  80.5 2.0 broadcast_select_fusion.1
  82.5 4.8 %collective-permute-start.2 = (bf16[128,2048]{1,0:T(8,128)(2,1)}, bf16[128,2048]{1,0:T(8,128)(2,1)}, u32[]{:S(2)}, u32[]{:S(2)}) collective-permute-start(bf16[128,2048]{1,0:T(8,128)(2,1)} %broadcast_select_fusion.1), channel_id=1, source_target_pairs={{0,1},{1,2},{2,3},{3,4},{4,5},{5,6},{6,7},{8,9},{9,10},{10,11},{11... | collective-permute-start | bytes 1572872 | tf_op jit(solution)/shard_map/ppermute | solution.py:11
  87.3 5.1 %gather_fusion.4 = bf16[128,2048]{1,0:T(8,128)(2,1)} fusion(bf16[1024,2048]{1,0:T(8,128)(2,1)} %bitcast.69, s32[1024]{0:T(1024)} %copy-done.6), kind=kCustom, calls=%fused_computation.4.clone | custom fusion | bytes 1049088 | tf_op jit(solution)/shard_map/jit(_take)/gather | solution.py:18
  92.4 2.0 broadcast_select_fusion
  94.4 1.5 collective-permute-start.3
  95.9 4.7 %constant_dynamic-update-slice_fusion.4 = bf16[1536,2048]{1,0:T(8,128)(2,1)} fusion(bf16[1,1,1024,2048]{3,2,1,0:T(8,128)(2,1)} %param.10), kind=kLoop, calls=%fused_computation.39 | loop fusion | bytes 8388608
  100.6 81.2 %all-reduce.3.cloned.1.call-done = f32[200,200]{0,1:T(8,128)} async-done(((f32[200,200]{0,1:T(8,128)}), f32[200,200]{0,1:T(8,128)}) %all-reduce.3.cloned.1.call-update) | async-done | bytes 160016 | tf_op jit(solution)/shard_map/psum | solution.py:46
  181.8 0.9 broadcast_multiply_fusion.1
  182.7 0.8 copy.17
  183.5 1.9 constant_dynamic-update-slice_fusion.3
  185.4 1.9 constant_dynamic-update-slice_fusion.2
  187.3 1.9 constant_dynamic-update-slice_fusion.1
  189.2 1.9 constant_dynamic-update-slice_fusion
  191.2 11.2 %convert_bitcast_fusion = bf16[1,1,1024,2048]{2,3,1,0:T(8,128)(2,1)} fusion(bf16[1536,2048]{1,0:T(8,128)(2,1)} %constant_dynamic-update-slice_fusion, bf16[1,1,1024,1536]{3,2,1,0:T(8,128)(2,1)S(1)} %copy-done), kind=kOutput, calls=%fused_computation.9 | convolution fusion | flops 6444548096 | bytes 13631488 | tf_op jit(solution)/shard_map/dot_general | solution.py:31
  202.4 6.4 %copy.16 = bf16[1,1,1024,2048]{3,2,1,0:T(8,128)(2,1)} copy(bf16[1,1,1024,2048]{2,3,1,0:T(8,128)(2,1)} %convert_bitcast_fusion) | data formatting | bytes 8388608
  208.8 25.5 %all-reduce.5.cloned.1.call-done = f32[200,256]{1,0:T(8,128)} async-done(((f32[200,256]{1,0:T(8,128)}), f32[200,256]{1,0:T(8,128)}) %all-reduce.5.cloned.1.call-update) | async-done | bytes 204816 | tf_op jit(solution)/shard_map/psum | solution.py:48
  234.3 1.6 broadcast_multiply_fusion
  (53 shorter events, 0.5 us)
Async XLA Ops:
  8.0 183.2 %copy-start = (bf16[1,1,1024,1536]{3,2,1,0:T(8,128)(2,1)S(1)}, bf16[1,1,1024,1536]{3,2,1,0:T(8,128)(2,1)}, u32[]{:S(2)}) copy-start(bf16[1,1,1024,1536]{3,2,1,0:T(8,128)(2,1)} %param.11) | copy-start | bytes 9437188
  8.0 23.1 %copy-start.2 = (s32[1,1,8,8]{3,2,1,0:T(8,128)S(1)}, s32[1,1,8,8]{3,2,1,0:T(8,128)}, u32[]{:S(2)}) copy-start(s32[1,1,8,8]{3,2,1,0:T(8,128)} %param.13) | copy-start | bytes 772
  8.0 173.8 %all-reduce.3.cloned.1.call-start = ((), (), s32[]{:S(2)}) async-start(), calls=%async_computation.1 | async-start | bytes 409600 | tf_op jit(solution)/shard_map/psum | solution.py:46
  9.0 10.9 %copy-start.11 = (pred[128]{0:T(512)(128)(4,1)}, pred[128]{0:T(512)(128)(4,1)S(1)}, u32[]{:S(2)}) copy-start(pred[128]{0:T(512)(128)(4,1)S(1)} %get-tuple-element.19) | copy-start | bytes 388
  9.0 10.9 %copy-start.13 = (pred[128]{0:T(512)(128)(4,1)}, pred[128]{0:T(512)(128)(4,1)S(1)}, u32[]{:S(2)}) copy-start(pred[128]{0:T(512)(128)(4,1)S(1)} %get-tuple-element.21) | copy-start | bytes 388
  9.0 16.3 %copy-start.9 = (pred[128]{0:T(512)(128)(4,1)}, pred[128]{0:T(512)(128)(4,1)S(1)}, u32[]{:S(2)}) copy-start(pred[128]{0:T(512)(128)(4,1)S(1)} %get-tuple-element.23) | copy-start | bytes 388
  9.0 30.2 %copy-start.7 = (pred[128]{0:T(512)(128)(4,1)}, pred[128]{0:T(512)(128)(4,1)S(1)}, u32[]{:S(2)}) copy-start(pred[128]{0:T(512)(128)(4,1)S(1)} %get-tuple-element.11) | copy-start | bytes 388
  9.0 3.9 %copy-start.3 = (s32[1024]{0:T(1024)}, s32[1024]{0:T(1024)S(1)}, u32[]{:S(2)}) copy-start(s32[1024]{0:T(1024)S(1)} %pad_clamp_fusion.4) | copy-start | bytes 12292
  13.0 18.8 %collective-permute-start.4 = (bf16[128,200]{1,0:T(8,128)(2,1)S(1)}, bf16[128,200]{1,0:T(8,128)(2,1)S(1)}, u32[]{:S(2)}, u32[]{:S(2)}) collective-permute-start(bf16[128,200]{1,0:T(8,128)(2,1)S(1)} %broadcast_select_fusion.7), channel_id=1, source_target_pairs={{0,8},{8,16},{16,24},{1,9},{9,17},{17,25},{2,10},{10,18},{18,26},{... | collective-permute-start | bytes 153608 | tf_op jit(solution)/shard_map/ppermute | solution.py:11
  17.9 1.9 copy-start.4
  19.9 12.5 %collective-permute-start.5 = (bf16[128,200]{1,0:T(8,128)(2,1)S(1)}, bf16[128,200]{1,0:T(8,128)(2,1)S(1)}, u32[]{:S(2)}, u32[]{:S(2)}) collective-permute-start(bf16[128,200]{1,0:T(8,128)(2,1)S(1)} %broadcast_select_fusion.6), channel_id=1, source_target_pairs={{8,0},{16,8},{24,16},{9,1},{17,9},{25,17},{10,2},{18,10},{26,18},{... | collective-permute-start | bytes 153608 | tf_op jit(solution)/shard_map/ppermute | solution.py:11
  21.2 1.9 copy-start.5
  23.2 9.9 %collective-permute-start.6 = (bf16[128,200]{1,0:T(8,128)(2,1)S(1)}, bf16[128,200]{1,0:T(8,128)(2,1)}, u32[]{:S(2)}, u32[]{:S(2)}) collective-permute-start(bf16[128,200]{1,0:T(8,128)(2,1)S(1)} %broadcast_select_fusion.5), channel_id=1, source_target_pairs={{0,1},{1,2},{2,3},{3,4},{4,5},{5,6},{6,7},{8,9},{9,10},{10,11},{11... | collective-permute-start | bytes 153608 | tf_op jit(solution)/shard_map/ppermute | solution.py:11
  25.3 3.9 %copy-start.6 = (s32[1024]{0:T(1024)}, s32[1024]{0:T(1024)S(1)}, u32[]{:S(2)}) copy-start(s32[1024]{0:T(1024)S(1)} %pad_clamp_fusion.1) | copy-start | bytes 12292
  27.9 6.6 %collective-permute-start.7 = (bf16[128,200]{1,0:T(8,128)(2,1)}, bf16[128,200]{1,0:T(8,128)(2,1)S(1)}, u32[]{:S(2)}, u32[]{:S(2)}) collective-permute-start(bf16[128,200]{1,0:T(8,128)(2,1)} %broadcast_select_fusion.4), channel_id=1, source_target_pairs={{1,0},{2,1},{3,2},{4,3},{5,4},{6,5},{7,6},{9,8},{10,9},{11,10},{12... | collective-permute-start | bytes 153608 | tf_op jit(solution)/shard_map/ppermute | solution.py:11
  45.2 3.7 %copy-start.1 = (bf16[1,1,1024,200]{2,3,1,0:T(8,128)(2,1)S(1)}, bf16[1,1,1024,200]{2,3,1,0:T(8,128)(2,1)}, u32[]{:S(2)}) copy-start(bf16[1,1,1024,200]{2,3,1,0:T(8,128)(2,1)} %param.14) | copy-start | bytes 1228804
  49.9 141.2 %reduce-scatter.2.cloned.1.call-start = ((), (), s32[]{:S(2)}) async-start(), calls=%async_computation.2 | async-start | bytes 1843200 | tf_op jit(solution)/shard_map/reduce_scatter | solution.py:47
  54.3 5.2 %copy-start.14 = (pred[128]{0:T(512)(128)(4,1)S(1)}, pred[128]{0:T(512)(128)(4,1)}, u32[]{:S(2)}) copy-start(pred[128]{0:T(512)(128)(4,1)} %copy-done.13) | copy-start | bytes 388
  54.3 180.0 %all-reduce.5.cloned.1.call-start = ((), (), s32[]{:S(2)}) async-start(), calls=%async_computation.3 | async-start | bytes 409600 | tf_op jit(solution)/shard_map/psum | solution.py:48
  54.4 17.6 %copy-start.12 = (pred[128]{0:T(512)(128)(4,1)S(1)}, pred[128]{0:T(512)(128)(4,1)}, u32[]{:S(2)}) copy-start(pred[128]{0:T(512)(128)(4,1)} %copy-done.11) | copy-start | bytes 388
  61.5 19.0 %copy-start.10 = (pred[128]{0:T(512)(128)(4,1)S(1)}, pred[128]{0:T(512)(128)(4,1)}, u32[]{:S(2)}) copy-start(pred[128]{0:T(512)(128)(4,1)} %copy-done.9) | copy-start | bytes 388
  61.5 122.0 %collective-permute-start = (bf16[128,2048]{1,0:T(8,128)(2,1)}, bf16[128,2048]{1,0:T(8,128)(2,1)}, u32[]{:S(2)}, u32[]{:S(2)}) collective-permute-start(bf16[128,2048]{1,0:T(8,128)(2,1)} %broadcast_select_fusion.3), channel_id=1, source_target_pairs={{0,8},{8,16},{16,24},{1,9},{9,17},{17,25},{2,10},{10,18},{18,26},{... | collective-permute-start | bytes 1572872 | tf_op jit(solution)/shard_map/ppermute | solution.py:11
  74.0 18.4 %copy-start.8 = (pred[128]{0:T(512)(128)(4,1)S(1)}, pred[128]{0:T(512)(128)(4,1)}, u32[]{:S(2)}) copy-start(pred[128]{0:T(512)(128)(4,1)} %copy-done.7) | copy-start | bytes 388
  74.0 111.4 %collective-permute-start.1 = (bf16[128,2048]{1,0:T(8,128)(2,1)}, bf16[128,2048]{1,0:T(8,128)(2,1)}, u32[]{:S(2)}, u32[]{:S(2)}) collective-permute-start(bf16[128,2048]{1,0:T(8,128)(2,1)} %broadcast_select_fusion.2), channel_id=1, source_target_pairs={{8,0},{16,8},{24,16},{9,1},{17,9},{25,17},{10,2},{18,10},{26,18},{... | collective-permute-start | bytes 1572872 | tf_op jit(solution)/shard_map/ppermute | solution.py:11
  82.5 104.8 %collective-permute-start.2 = (bf16[128,2048]{1,0:T(8,128)(2,1)}, bf16[128,2048]{1,0:T(8,128)(2,1)}, u32[]{:S(2)}, u32[]{:S(2)}) collective-permute-start(bf16[128,2048]{1,0:T(8,128)(2,1)} %broadcast_select_fusion.1), channel_id=1, source_target_pairs={{0,1},{1,2},{2,3},{3,4},{4,5},{5,6},{6,7},{8,9},{9,10},{10,11},{11... | collective-permute-start | bytes 1572872 | tf_op jit(solution)/shard_map/ppermute | solution.py:11
  94.4 94.8 %collective-permute-start.3 = (bf16[128,2048]{1,0:T(8,128)(2,1)}, bf16[128,2048]{1,0:T(8,128)(2,1)}, u32[]{:S(2)}, u32[]{:S(2)}) collective-permute-start(bf16[128,2048]{1,0:T(8,128)(2,1)} %broadcast_select_fusion), channel_id=1, source_target_pairs={{1,0},{2,1},{3,2},{4,3},{5,4},{6,5},{7,6},{9,8},{10,9},{11,10},{12... | collective-permute-start | bytes 1572872 | tf_op jit(solution)/shard_map/ppermute | solution.py:11
Sparse Core Ops, SparseCore 0:
  50.0 131.7 all-reduce.2
Sparse Core Ops, SparseCore 1:
  54.4 39.1 reduce-scatter.1
  191.2 43.0 all-reduce.4
where the time goes:
time: 245 us; the launch traced here: 243 us
  waiting for transfers between devices  107 us (44%)
  local copies, waits for them, and re-layouts  64.9 us (26%)
  starting transfers between devices  22.6 us (9%)
  matrix products  20.2 us (8%)
  between operations  15.8 us (6%)
  other arithmetic  13 us (5%)
    psum x1, waiting for transfers between devices, local(): galerkin = lax.psum(galerkin_term, ('grp', 'sub')) * scaling  81.2 us
    psum x1, waiting for transfers between devices, local(): owned = lax.psum(partial_rhs, 'grp')  25.5 us
    unnamed x41, local copies, waits for them, and re-layouts  24.4 us
    ppermute x8, starting transfers between devices, passed_along(): return lax.ppermute(x, axis, pairs)  22.5 us
    gather x4, local copies, waits for them, and re-layouts, local(): jnp.take(resid_own, rows_here[face_index], axis=0)  20.5 us
    dot_general x1, matrix products, local(): jnp.dot(inverse_blocks[0, 0], resid_ext, preferred_element_type=jnp.float32)  11.2 us
    gather x2, local copies, waits for them, and re-layouts, local(): picked = jnp.take(blocks, column_blocks[0, 0], axis=0)  9.99 us
    select_n x4, other arithmetic, local(): jnp.take(resid_own, rows_here[face_index], axis=0)  7.93 us
  transfers between devices with their start and end apart: 11, of which 2 were waited for; matrix products, arithmetic and copies ran while one was open for 31% of the time, Pallas kernels for 0%

commit v1 on v0

--- a/solution.py
+++ b/solution.py
@@ -43,7 +43,11 @@
     group_count = lax.axis_size("grp")
     sub_count = lax.axis_size("sub")
     scaling = 1.0 / math.sqrt(resid_own.shape[0] * group_count * sub_count)
-    galerkin = lax.psum(galerkin_term, ("grp", "sub")) * scaling
+
+    def _push_slabs(base_x):
+        return lax.all_gather(base_x, ("grp", "sub")).sum(axis=0)
+
+    galerkin = _push_slabs(galerkin_term) * scaling
     partial_rhs = lax.psum_scatter(rhs_term, "sub", scatter_dimension=1, tiled=True)
     owned = lax.psum(partial_rhs, "grp")
     coarse_rhs = owned * scaling

time: 245 us -> 173 us (0.71)
  waiting for transfers between devices: 107 us -> 18.6 us
  other arithmetic: 13 us -> 27.8 us
    psum x1 -> x0, waiting for transfers between devices: 81.2 us -> none  [local(): galerkin = lax.psum(galerkin_term, ('grp', 'sub')) * scaling]
    psum x1, waiting for transfers between devices: 25.5 us -> 0.01 us  [local(): owned = lax.psum(partial_rhs, 'grp')]
    all_gather x0 -> x1, waiting for transfers between devices: none -> 17.3 us  [_push_slabs(): return lax.all_gather(base_x, ('grp', 'sub')).sum(axis=0)]
    select_n x4, other arithmetic: 0.97 us -> 6.2 us  [local(): jnp.take(basis_own, rows_here[face_index], axis=0)]
    gather x4, other arithmetic: 0.02 us -> 4.31 us
    unnamed x41 -> x24, local copies, waits for them, and re-layouts: 24.4 us -> 20.5 us
    reduce_sum x0 -> x1, other arithmetic: none -> 3.31 us  [_push_slabs(): return lax.all_gather(base_x, ('grp', 'sub')).sum(axis=0)]
    gather x4, local copies, waits for them, and re-layouts: 7.46 us -> 10.4 us  [local(): jnp.take(basis_own, rows_here[face_index], axis=0)]
  transfers between devices with their start and end apart: 11 -> 11, of which waited for: 2 -> 2; matrix products, arithmetic and copies ran while one was open for 31% -> 61% of each run, Pallas kernels for 0% -> 0%
where the time goes in v1:
time: 173 us; the launch traced here: 171 us
  local copies, waits for them, and re-layouts  66.1 us (38%)
  other arithmetic  27.8 us (16%)
  starting transfers between devices  23.1 us (13%)
  matrix products  19.8 us (11%)
  waiting for transfers between devices  18.6 us (11%)
  between operations  15.7 us (9%)
    ppermute x8, starting transfers between devices, passed_along(): return lax.ppermute(x, axis, pairs)  23 us
    gather x4, local copies, waits for them, and re-layouts, local(): jnp.take(resid_own, rows_here[face_index], axis=0)  20.6 us
    unnamed x24, local copies, waits for them, and re-layouts  20.5 us
    all_gather x1, waiting for transfers between devices, _push_slabs(): return lax.all_gather(base_x, ('grp', 'sub')).sum(axis=0)  17.3 us
    gather x4, local copies, waits for them, and re-layouts, local(): jnp.take(basis_own, rows_here[face_index], axis=0)  10.4 us
    gather x2, local copies, waits for them, and re-layouts, local(): picked = jnp.take(blocks, column_blocks[0, 0], axis=0)  10.1 us
    dot_general x1, matrix products, local(): jnp.dot(inverse_blocks[0, 0], resid_ext, preferred_element_type=jnp.float32)  8.69 us
    select_n x4, other arithmetic, local(): jnp.take(resid_own, rows_here[face_index], axis=0)  7.14 us
  transfers between devices with their start and end apart: 11, of which 2 were waited for; matrix products, arithmetic and copies ran while one was open for 61% of the time, Pallas kernels for 0%

profile of v1, /device:TPU:0, one launch (start us, length us, event | category | flops | bytes accessed | tf_op | source)
XLA Modules:
  0.0 171.1 jit_solution(12750319335559022073)
XLA Ops:
  8.1 4.7 %fusion.23 = f32[200,2048]{1,0:T(8,128)} fusion(bf16[1,1,1024,200]{2,3,1,0:T(8,128)(2,1)} %param.14, bf16[1,1,1024,2048]{3,2,1,0:T(8,128)(2,1)} %param.10), kind=kOutput, calls=%fused_computation.26 | convolution fusion | flops 838860800 | bytes 6242304 | tf_op jit(solution)/shard_map/rc,rk->ck/dot_general | solution.py:24
  13.9 1.4 compare_and_fusion.1
  15.9 2.6 %gather_fusion.5 = bf16[128,200]{1,0:T(8,128)(2,1)} fusion(bf16[1024,200]{1,0:T(8,128)(2,1)} %bitcast.71, s32[1024]{0:T(1024)} %pad_clamp_fusion.4), kind=kCustom, calls=%fused_computation.1.clone | custom fusion | bytes 102912 | tf_op jit(solution)/shard_map/jit(_take)/gather | solution.py:19
  18.5 1.6 broadcast_select_fusion.7
  20.1 5.5 %collective-permute-start.4 = (bf16[128,200]{1,0:T(8,128)(2,1)}, bf16[128,200]{1,0:T(8,128)(2,1)}, u32[]{:S(2)}, u32[]{:S(2)}) collective-permute-start(bf16[128,200]{1,0:T(8,128)(2,1)} %broadcast_select_fusion.7), channel_id=1, source_target_pairs={{0,8},{8,16},{16,24},{1,9},{9,17},{17,25},{2,10},{10,18},{18,26},{... | collective-permute-start | bytes 153608 | tf_op jit(solution)/shard_map/ppermute | solution.py:11
  25.5 1.2 pad_clamp_fusion.3
  26.8 2.6 %gather_fusion.6 = bf16[128,200]{1,0:T(8,128)(2,1)} fusion(bf16[1024,200]{1,0:T(8,128)(2,1)} %bitcast.72, s32[1024]{0:T(1024)} %pad_clamp_fusion.3), kind=kCustom, calls=%fused_computation.5.clone | custom fusion | bytes 102912 | tf_op jit(solution)/shard_map/jit(_take)/gather | solution.py:19
  29.4 1.6 broadcast_select_fusion.6
  31.0 1.3 collective-permute-start.5
  32.3 1.2 pad_clamp_fusion.2
  33.5 2.6 %gather_fusion.7 = bf16[128,200]{1,0:T(8,128)(2,1)} fusion(bf16[1024,200]{1,0:T(8,128)(2,1)} %bitcast.73, s32[1024]{0:T(1024)} %pad_clamp_fusion.2), kind=kCustom, calls=%fused_computation.6.clone | custom fusion | bytes 102912 | tf_op jit(solution)/shard_map/jit(_take)/gather | solution.py:19
  36.1 1.5 broadcast_select_fusion.5
  37.6 2.1 %collective-permute-start.6 = (bf16[128,200]{1,0:T(8,128)(2,1)}, bf16[128,200]{1,0:T(8,128)(2,1)}, u32[]{:S(2)}, u32[]{:S(2)}) collective-permute-start(bf16[128,200]{1,0:T(8,128)(2,1)} %broadcast_select_fusion.5), channel_id=1, source_target_pairs={{0,1},{1,2},{2,3},{3,4},{4,5},{5,6},{6,7},{8,9},{9,10},{10,11},{11... | collective-permute-start | bytes 153608 | tf_op jit(solution)/shard_map/ppermute | solution.py:11
  39.7 1.3 pad_clamp_fusion.1
  40.9 2.6 %gather_fusion.8 = bf16[128,200]{1,0:T(8,128)(2,1)} fusion(bf16[1024,200]{1,0:T(8,128)(2,1)} %bitcast.74, s32[1024]{0:T(1024)} %pad_clamp_fusion.1), kind=kCustom, calls=%fused_computation.7.clone | custom fusion | bytes 102912 | tf_op jit(solution)/shard_map/jit(_take)/gather | solution.py:19
  43.5 1.5 broadcast_select_fusion.4
  45.1 1.3 collective-permute-start.7
  46.4 1.3 compare_select_fusion
  47.7 1.3 reshape.130
  48.9 1.3 compare_and_fusion
  50.2 1.9 %constant_dynamic-update-slice_fusion.9 = bf16[1536,200]{1,0:T(8,128)(2,1)} fusion(bf16[1,1,1024,200]{3,2,1,0:T(8,128)(2,1)} %copy.16), kind=kLoop, calls=%fused_computation.44 | loop fusion | bytes 933888
  53.3 1.5 constant_dynamic-update-slice_fusion.8
  54.7 1.5 constant_dynamic-update-slice_fusion.7
  56.2 1.5 constant_dynamic-update-slice_fusion.6
  57.6 1.5 constant_dynamic-update-slice_fusion.5
  59.1 4.1 %gather_fusion = bf16[64,128,200]{2,1,0:T(8,128)(2,1)} fusion(bf16[12,128,200]{2,1,0:T(8,128)(2,1)} %bitcast.10, s32[1024]{0:T(1024)} %pad_clamp_fusion), kind=kCustom, calls=%fused_computation.8 | custom fusion | bytes 6553856 | tf_op jit(solution)/shard_map/jit(_take)/gather | solution.py:37
  63.2 6.1 %copy.17 = bf16[64,128,200]{1,2,0:T(8,128)(2,1)} copy(bf16[64,128,200]{2,1,0:T(8,128)(2,1)} %gather_fusion) | data formatting | bytes 6553600 | tf_op jit(solution)/shard_map/jit(_take)/gather | solution.py:37
  69.3 4.4 %fusion.16 = bf16[8,25,8,128]{3,2,1,0:T(8,128)(2,1)} fusion(bf16[1,1,8,8,128,128]{5,4,3,2,1,0:T(8,128)(2,1)} %param.12, bf16[8,8,128,200]{2,3,1,0:T(8,128)(2,1)} %bitcast.76, pred[8,8]{1,0:T(8,128)(4,1)} %compare_and_fusion), kind=kOutput, calls=%fused_computation.18 | convolution fusion | flops 421273600 | bytes 5783616 | tf_op jit(solution)/shard_map/bjtu,bjuc->btc/dot_general | solution.py:38
  73.7 2.0 %convolution_bitcast_fusion = f32[200,200]{0,1:T(8,128)} fusion(bf16[8,25,8,128]{3,2,1,0:T(8,128)(2,1)} %fusion.16, bf16[1,1,1024,200]{2,3,1,0:T(8,128)(2,1)S(1)} %copy-done.1), kind=kOutput, calls=%fused_computation.19 | convolution fusion | flops 81920000 | bytes 979200 | tf_op jit(solution)/shard_map/rc,rd->cd/dot_general | solution.py:42
  75.7 1.7 %copy.19 = f32[200,200]{1,0:T(8,128)} copy(f32[200,200]{0,1:T(8,128)} %convolution_bitcast_fusion) | data formatting | bytes 320000 | tf_op jit(solution)/shard_map/rc,rd->cd/dot_general | solution.py:42
  77.5 5.1 %gather_fusion.1 = bf16[128,2048]{1,0:T(8,128)(2,1)} fusion(bf16[1024,2048]{1,0:T(8,128)(2,1)} %bitcast.67, s32[1024]{0:T(1024)} %pad_clamp_fusion.4), kind=kCustom, calls=%fused_computation.clone | custom fusion | bytes 1049088 | tf_op jit(solution)/shard_map/jit(_take)/gather | solution.py:18
  82.6 2.0 %broadcast_select_fusion.3 = bf16[128,2048]{1,0:T(8,128)(2,1)} fusion(bf16[128,2048]{1,0:T(8,128)(2,1)} %gather_fusion.1, pred[128]{0:T(512)(128)(4,1)S(1)} %copy-done.5), kind=kLoop, calls=%fused_computation.23 | loop fusion | flops 262144 | bytes 1048704 | tf_op jit(solution)/shard_map/jit(_take)/select_n | solution.py:18
  84.5 5.3 %collective-permute-start = (bf16[128,2048]{1,0:T(8,128)(2,1)}, bf16[128,2048]{1,0:T(8,128)(2,1)}, u32[]{:S(2)}, u32[]{:S(2)}) collective-permute-start(bf16[128,2048]{1,0:T(8,128)(2,1)} %broadcast_select_fusion.3), channel_id=1, source_target_pairs={{0,8},{8,16},{16,24},{1,9},{9,17},{17,25},{2,10},{10,18},{18,26},{... | collective-permute-start | bytes 1572872 | tf_op jit(solution)/shard_map/ppermute | solution.py:11
  89.9 5.2 %gather_fusion.2 = bf16[128,2048]{1,0:T(8,128)(2,1)} fusion(bf16[1024,2048]{1,0:T(8,128)(2,1)} %bitcast.68, s32[1024]{0:T(1024)} %pad_clamp_fusion.3), kind=kCustom, calls=%fused_computation.2.clone | custom fusion | bytes 1049088 | tf_op jit(solution)/shard_map/jit(_take)/gather | solution.py:18
  95.1 2.0 %broadcast_select_fusion.2 = bf16[128,2048]{1,0:T(8,128)(2,1)} fusion(bf16[128,2048]{1,0:T(8,128)(2,1)} %gather_fusion.2, pred[128]{0:T(512)(128)(4,1)S(1)} %copy-done.4), kind=kLoop, calls=%fused_computation.22 | loop fusion | flops 262144 | bytes 1048704 | tf_op jit(solution)/shard_map/jit(_take)/select_n | solution.py:18
  97.1 1.4 collective-permute-start.1
  98.5 5.2 %gather_fusion.3 = bf16[128,2048]{1,0:T(8,128)(2,1)} fusion(bf16[1024,2048]{1,0:T(8,128)(2,1)} %bitcast.69, s32[1024]{0:T(1024)} %pad_clamp_fusion.2), kind=kCustom, calls=%fused_computation.3.clone | custom fusion | bytes 1049088 | tf_op jit(solution)/shard_map/jit(_take)/gather | solution.py:18
  103.7 2.0 %broadcast_select_fusion.1 = bf16[128,2048]{1,0:T(8,128)(2,1)} fusion(bf16[128,2048]{1,0:T(8,128)(2,1)} %gather_fusion.3, pred[128]{0:T(512)(128)(4,1)S(1)} %copy-done.3), kind=kLoop, calls=%fused_computation.21 | loop fusion | flops 262144 | bytes 1048704 | tf_op jit(solution)/shard_map/jit(_take)/select_n | solution.py:18
  105.8 4.7 %collective-permute-start.2 = (bf16[128,2048]{1,0:T(8,128)(2,1)}, bf16[128,2048]{1,0:T(8,128)(2,1)}, u32[]{:S(2)}, u32[]{:S(2)}) collective-permute-start(bf16[128,2048]{1,0:T(8,128)(2,1)} %broadcast_select_fusion.1), channel_id=1, source_target_pairs={{0,1},{1,2},{2,3},{3,4},{4,5},{5,6},{6,7},{8,9},{9,10},{10,11},{11... | collective-permute-start | bytes 1572872 | tf_op jit(solution)/shard_map/ppermute | solution.py:11
  110.4 5.1 %gather_fusion.4 = bf16[128,2048]{1,0:T(8,128)(2,1)} fusion(bf16[1024,2048]{1,0:T(8,128)(2,1)} %bitcast.70, s32[1024]{0:T(1024)} %pad_clamp_fusion.1), kind=kCustom, calls=%fused_computation.4.clone | custom fusion | bytes 1049088 | tf_op jit(solution)/shard_map/jit(_take)/gather | solution.py:18
  116.7 1.5 collective-permute-start.3
  118.1 2.5 %constant_dynamic-update-slice_fusion.4 = bf16[1536,2048]{1,0:T(8,128)(2,1)S(1)} fusion(bf16[1,1,1024,2048]{3,2,1,0:T(8,128)(2,1)} %param.10), kind=kLoop, calls=%fused_computation.39 | loop fusion | bytes 8388608
  121.7 1.3 collective-permute-done.1
  125.3 8.7 %convert_bitcast_fusion = bf16[1,1,1024,2048]{2,3,1,0:T(8,128)(2,1)} fusion(bf16[1536,2048]{1,0:T(8,128)(2,1)S(1)} %constant_dynamic-update-slice_fusion, bf16[1,1,1024,1536]{3,2,1,0:T(8,128)(2,1)S(1)} %copy-done), kind=kOutput, calls=%fused_computation.9 | convolution fusion | flops 6444548096 | bytes 13631488 | tf_op jit(solution)/shard_map/dot_general | solution.py:31
  134.0 6.5 %copy.21 = bf16[1,1,1024,2048]{3,2,1,0:T(8,128)(2,1)} copy(bf16[1,1,1024,2048]{2,3,1,0:T(8,128)(2,1)} %convert_bitcast_fusion) | data formatting | bytes 8388608
  140.5 1.6 broadcast_multiply_fusion
  142.1 17.3 %all-gather.3.cloned.1.call-done = f32[6400,200]{1,0:T(8,128)} async-done(((f32[200,200]{1,0:T(8,128)}), f32[6400,200]{1,0:T(8,128)}) %all-gather.3.cloned.1.call-update) | async-done | bytes 5120016 | tf_op jit(solution)/shard_map/all_gather | solution.py:48
  159.4 3.3 %reduce_sum.9 = f32[200,200]{1,0:T(8,128)S(1)} reduce(f32[32,200,200]{2,1,0:T(8,128)} %bitcast.75, f32[]{:T(128)} %constant.30.clone.1), dimensions={0}, to_apply=%region_0.3 | reduce | flops 1240000 | bytes 5280004 | tf_op jit(solution)/shard_map/reduce_sum | solution.py:48
  (38 shorter events, 8.4 us)
Async XLA Ops:
  8.0 117.3 %copy-start = (bf16[1,1,1024,1536]{3,2,1,0:T(8,128)(2,1)S(1)}, bf16[1,1,1024,1536]{3,2,1,0:T(8,128)(2,1)}, u32[]{:S(2)}) copy-start(bf16[1,1,1024,1536]{3,2,1,0:T(8,128)(2,1)} %param.11) | copy-start | bytes 9437188
  8.0 4.8 %copy-start.1 = (bf16[1,1,1024,200]{2,3,1,0:T(8,128)(2,1)S(1)}, bf16[1,1,1024,200]{2,3,1,0:T(8,128)(2,1)}, u32[]{:S(2)}) copy-start(bf16[1,1,1024,200]{2,3,1,0:T(8,128)(2,1)} %param.14) | copy-start | bytes 1228804
  8.0 65.6 %reduce-scatter.2.cloned.1.call-start = ((), (), s32[]{:S(2)}) async-start(), calls=%async_computation.1 | async-start | bytes 1843200 | tf_op jit(solution)/shard_map/reduce_scatter | solution.py:51
  12.8 127.7 %all-reduce.2.cloned.1.call-start = ((), (), s32[]{:S(2)}) async-start(), calls=%async_computation.2 | async-start | bytes 409600 | tf_op jit(solution)/shard_map/psum | solution.py:52
  20.1 33.2 %collective-permute-start.4 = (bf16[128,200]{1,0:T(8,128)(2,1)}, bf16[128,200]{1,0:T(8,128)(2,1)}, u32[]{:S(2)}, u32[]{:S(2)}) collective-permute-start(bf16[128,200]{1,0:T(8,128)(2,1)} %broadcast_select_fusion.7), channel_id=1, source_target_pairs={{0,8},{8,16},{16,24},{1,9},{9,17},{17,25},{2,10},{10,18},{18,26},{... | collective-permute-start | bytes 153608 | tf_op jit(solution)/shard_map/ppermute | solution.py:11
  31.0 23.7 %collective-permute-start.5 = (bf16[128,200]{1,0:T(8,128)(2,1)}, bf16[128,200]{1,0:T(8,128)(2,1)}, u32[]{:S(2)}, u32[]{:S(2)}) collective-permute-start(bf16[128,200]{1,0:T(8,128)(2,1)} %broadcast_select_fusion.6), channel_id=1, source_target_pairs={{8,0},{16,8},{24,16},{9,1},{17,9},{25,17},{10,2},{18,10},{26,18},{... | collective-permute-start | bytes 153608 | tf_op jit(solution)/shard_map/ppermute | solution.py:11
  37.6 18.6 %collective-permute-start.6 = (bf16[128,200]{1,0:T(8,128)(2,1)}, bf16[128,200]{1,0:T(8,128)(2,1)}, u32[]{:S(2)}, u32[]{:S(2)}) collective-permute-start(bf16[128,200]{1,0:T(8,128)(2,1)} %broadcast_select_fusion.5), channel_id=1, source_target_pairs={{0,1},{1,2},{2,3},{3,4},{4,5},{5,6},{6,7},{8,9},{9,10},{10,11},{11... | collective-permute-start | bytes 153608 | tf_op jit(solution)/shard_map/ppermute | solution.py:11
  45.1 12.6 %collective-permute-start.7 = (bf16[128,200]{1,0:T(8,128)(2,1)}, bf16[128,200]{1,0:T(8,128)(2,1)}, u32[]{:S(2)}, u32[]{:S(2)}) collective-permute-start(bf16[128,200]{1,0:T(8,128)(2,1)} %broadcast_select_fusion.4), channel_id=1, source_target_pairs={{1,0},{2,1},{3,2},{4,3},{5,4},{6,5},{7,6},{9,8},{10,9},{11,10},{12... | collective-permute-start | bytes 153608 | tf_op jit(solution)/shard_map/ppermute | solution.py:11
  73.7 85.7 %all-gather.3.cloned.1.call-start = ((), (), s32[]{:S(2)}) async-start(), calls=%async_computation.3 | async-start | bytes 6758400 | tf_op jit(solution)/shard_map/all_gather | solution.py:48
  75.7 6.9 %copy-start.5 = (pred[128]{0:T(512)(128)(4,1)S(1)}, pred[128]{0:T(512)(128)(4,1)}, u32[]{:S(2)}) copy-start(pred[128]{0:T(512)(128)(4,1)} %get-tuple-element.24) | copy-start | bytes 388
  77.5 17.6 %copy-start.4 = (pred[128]{0:T(512)(128)(4,1)S(1)}, pred[128]{0:T(512)(128)(4,1)}, u32[]{:S(2)}) copy-start(pred[128]{0:T(512)(128)(4,1)} %get-tuple-element.22) | copy-start | bytes 388
  84.5 19.2 %copy-start.3 = (pred[128]{0:T(512)(128)(4,1)S(1)}, pred[128]{0:T(512)(128)(4,1)}, u32[]{:S(2)}) copy-start(pred[128]{0:T(512)(128)(4,1)} %get-tuple-element.26) | copy-start | bytes 388
  84.5 36.1 %collective-permute-start = (bf16[128,2048]{1,0:T(8,128)(2,1)}, bf16[128,2048]{1,0:T(8,128)(2,1)}, u32[]{:S(2)}, u32[]{:S(2)}) collective-permute-start(bf16[128,2048]{1,0:T(8,128)(2,1)} %broadcast_select_fusion.3), channel_id=1, source_target_pairs={{0,8},{8,16},{16,24},{1,9},{9,17},{17,25},{2,10},{10,18},{18,26},{... | collective-permute-start | bytes 1572872 | tf_op jit(solution)/shard_map/ppermute | solution.py:11
  97.1 18.4 %copy-start.2 = (pred[128]{0:T(512)(128)(4,1)S(1)}, pred[128]{0:T(512)(128)(4,1)}, u32[]{:S(2)}) copy-start(pred[128]{0:T(512)(128)(4,1)} %get-tuple-element.14) | copy-start | bytes 388
  97.1 25.9 %collective-permute-start.1 = (bf16[128,2048]{1,0:T(8,128)(2,1)}, bf16[128,2048]{1,0:T(8,128)(2,1)}, u32[]{:S(2)}, u32[]{:S(2)}) collective-permute-start(bf16[128,2048]{1,0:T(8,128)(2,1)} %broadcast_select_fusion.2), channel_id=1, source_target_pairs={{8,0},{16,8},{24,16},{9,1},{17,9},{25,17},{10,2},{18,10},{26,18},{... | collective-permute-start | bytes 1572872 | tf_op jit(solution)/shard_map/ppermute | solution.py:11
  105.8 18.4 %collective-permute-start.2 = (bf16[128,2048]{1,0:T(8,128)(2,1)}, bf16[128,2048]{1,0:T(8,128)(2,1)}, u32[]{:S(2)}, u32[]{:S(2)}) collective-permute-start(bf16[128,2048]{1,0:T(8,128)(2,1)} %broadcast_select_fusion.1), channel_id=1, source_target_pairs={{0,1},{1,2},{2,3},{3,4},{4,5},{5,6},{6,7},{8,9},{9,10},{10,11},{11... | collective-permute-start | bytes 1572872 | tf_op jit(solution)/shard_map/ppermute | solution.py:11
  116.7 8.6 %collective-permute-start.3 = (bf16[128,2048]{1,0:T(8,128)(2,1)S(1)}, bf16[128,2048]{1,0:T(8,128)(2,1)S(1)}, u32[]{:S(2)}, u32[]{:S(2)}) collective-permute-start(bf16[128,2048]{1,0:T(8,128)(2,1)S(1)} %broadcast_select_fusion), channel_id=1, source_target_pairs={{1,0},{2,1},{3,2},{4,3},{5,4},{6,5},{7,6},{9,8},{10,9},{11,10},{12... | collective-permute-start | bytes 1572872 | tf_op jit(solution)/shard_map/ppermute | solution.py:11
Sparse Core Ops, SparseCore 0:
  12.9 37.5 reduce-scatter.1
  73.8 50.4 all-reduce.1
Sparse Core Ops, SparseCore 1:
  77.6 81.7 all-gather.2
